TPU v7x, 512 devices: a whole 4x4x16 slice. The times are simulated.
512 devices in a mesh: sec: 8 (over x, core), xy: 64 (over y, z).
Axes of the slice: x: 4, y: 4, z: 16, core: 2. Of those that a mesh axis runs over, the one named last changes fastest.
Arguments:
- source: bfloat16 [8, 32768, 1024], P('sec', 'xy'), may hold values from -6 to 6
- coarse: int32 [8, 2, 128], P('sec', None, 'xy'), may hold values from -1 to 1, as said below
- fraction: float32 [8, 2, 128], P('sec', None, 'xy'), may hold values from 0.25 to 0.75
- kernel_one: float32 [3, 3, 3], replicated, may hold values from -1.25 to 1.25
- kernel_two: float32 [3, 3, 3], replicated, may hold values from -1.25 to 1.25
Outputs:
- denoised: bfloat16 [8, 1024, 32768], P(None, 'xy', 'sec')
Inputs may be any that keep to these rules, and one draw needn't show every extreme that they name: Destination block (r, c) reads source block (r + coarse[z, 0, b], c + coarse[z, 1, b]); c + coarse[z, 1, b] always lies in 0 to 1. Among the 2 blocks of one block row of a section, at most one has a row offset of -1 and at most one has +1.
All inputs are finite; a program needn't handle non-finite values.
Results may differ from a plain program's by a relative error of at most 0.003.
The roundings to bfloat16 on the way count: a program that leaves them out, or rounds other values in their place, can miss the bound.
Values may be sent and summed in bfloat16 or wider, within the bound.
No kernel may reach another device: no remote copies, remote signals or barrier semaphores. Data moves between devices by JAX's collectives and lax.ppermute only.
A program may use at most 128 MiB of HBM per device.

v0:
```python
import jax
import jax.numpy as jnp
from jax import lax
from jax.sharding import PartitionSpec as P


def from_behind(value, axis, steps):
    count = lax.axis_size(axis)
    first, last = (max(0, -steps), min(count, count - steps))
    return lax.ppermute(value, axis, [(source, source + steps) for source in range(first, last)])


def with_halo(x, sides, width):
    for axis, dim in sides:
        size, length = (lax.axis_size(axis), x.shape[dim])
        up = [(i, (i + 1) % size) for i in range(size - 1)]
        down = [(j, i) for i, j in up]
        last = lax.slice_in_dim(x, length - width, length, axis=dim)
        first = lax.slice_in_dim(x, 0, width, axis=dim)
        before = lax.ppermute(last, axis, up)
        after = lax.ppermute(first, axis, down)
        x = jnp.concatenate([before, x, after], axis=dim)
    return x


def interpolation(shift, edge):
    row_index = lax.broadcasted_iota(jnp.int32, (edge, edge), 0)
    col_index = lax.broadcasted_iota(jnp.int32, (edge, edge), 1)
    offset = col_index - row_index
    amount = shift[..., None, None]
    w_before = ((-0.5 * amount + 1.0) * amount - 0.5) * amount
    w_center = (1.5 * amount - 2.5) * amount * amount + 1.0
    w_after = ((-1.5 * amount + 2.0) * amount + 0.5) * amount
    w_beyond = (0.5 * amount - 0.5) * amount * amount
    matrix = jnp.where(offset == -1, w_before, 0.0) + jnp.where(offset == 0, w_center, 0.0)
    matrix = matrix + jnp.where(offset == 1, w_after, 0.0) + jnp.where(offset == 2, w_beyond, 0.0)
    return matrix.astype(jnp.bfloat16)


def pad_sections(volume):
    return jnp.pad(volume, ((1, 1), (0, 0), (0, 0)))


def stencil(padded, kernel, depth, cols_out, rows_out):
    running = jnp.zeros((depth, cols_out, rows_out), jnp.float32)
    for tap_z in range(3):
        for tap_x in range(3):
            for tap_y in range(3):
                window = padded[
                    tap_z : tap_z + depth, tap_x : tap_x + cols_out, tap_y : tap_y + rows_out
                ]
                running = running + kernel[tap_z, tap_x, tap_y] * window
    return running


def body(source, coarse, fraction, kernel_one, kernel_two):
    sections_dev, edge, width = source.shape
    columns = width // edge
    row_shift = coarse[:, 0, :]
    col_shift = coarse[:, 1, :]
    target = lax.broadcasted_iota(jnp.int32, (sections_dev, columns, columns), 1)
    anchor = lax.broadcasted_iota(jnp.int32, (sections_dev, columns, columns), 2)
    from_above = from_behind(source, "xy", 1)
    from_below = from_behind(source, "xy", -1)
    stacked = jnp.stack([from_above, source, from_below]).reshape(
        3, sections_dev, edge, columns, edge
    )
    level = lax.broadcasted_iota(jnp.int32, (3, sections_dev, columns, columns), 0)
    choose = (row_shift[None, :, :, None] + 1 == level) & (
        target[None] + col_shift[None, :, :, None] == anchor[None]
    )
    picked = jnp.einsum(
        "ksnm,ksimj->snij", choose.astype(jnp.bfloat16), stacked, preferred_element_type=jnp.float32
    ).astype(jnp.bfloat16)
    row_matrix = interpolation(fraction[:, 0, :], edge)
    col_matrix = interpolation(fraction[:, 1, :], edge)
    rows_warped = jnp.einsum(
        "snij,snjk->snik", row_matrix, picked, preferred_element_type=jnp.float32
    ).astype(jnp.bfloat16)
    warped = jnp.einsum(
        "sncj,snrj->sncr", col_matrix, rows_warped, preferred_element_type=jnp.float32
    ).astype(jnp.bfloat16)
    aligned_strip = warped.reshape(sections_dev, width, edge)
    group_data = lax.all_to_all(
        lax.all_to_all(aligned_strip, "xy", split_axis=1, concat_axis=2, tiled=True),
        "sec",
        split_axis=2,
        concat_axis=0,
        tiled=True,
    )
    sections_all, group_cols, group_rows = group_data.shape
    rim_one = with_halo(group_data, (("sec", 2), ("xy", 1)), 1)
    first_pass = jnp.maximum(
        stencil(
            pad_sections(rim_one.astype(jnp.float32)),
            kernel_one,
            sections_all,
            group_cols,
            group_rows,
        ),
        0.0,
    ).astype(jnp.bfloat16)
    rim_two = with_halo(first_pass, (("sec", 2), ("xy", 1)), 1)
    second = stencil(
        pad_sections(rim_two.astype(jnp.float32)), kernel_two, sections_all, group_cols, group_rows
    )
    return (second + group_data.astype(jnp.float32)).astype(jnp.bfloat16)


def solution(mesh):
    placed = (P("sec", "xy", None), P("sec", None, "xy"), P("sec", None, "xy"), P(), P())
    return jax.shard_map(
        body, mesh=mesh, in_specs=placed, out_specs=P(None, "xy", "sec"), check_vma=False
    )
```

profile of v0, /device:TPU:9, one launch (start us, length us, event | category | flops | bytes accessed | tf_op | source)
XLA Modules:
  0.0 503.7 jit_solution(17445958585612541648)
XLA Ops:
  0.0 3.7 collective-permute-start
  3.7 9.4 %collective-permute-start.1 = (bf16[1,512,1024]{2,1,0:T(8,128)(2,1)}, bf16[1,512,1024]{2,1,0:T(8,128)(2,1)S(1)}, u32[]{:S(2)}, u32[]{:S(2)}) collective-permute-start(bf16[1,512,1024]{2,1,0:T(8,128)(2,1)} %param.5), channel_id=1, source_target_pairs={{1,0},{2,1},{3,2},{4,3},{5,4},{6,5},{7,6},{8,7},{9,8},{10,9},{11,1... | collective-permute-start | bytes 3145736 | tf_op jit(solution)/shard_map/ppermute | solution.py:10
  13.1 0.9 fusion.109
  13.9 1.8 stack.13
  15.8 1.0 fusion.111
  16.8 0.0 copy-done.8
  16.8 0.1 iota_compare_fusion.1
  16.8 0.1 fusion.122
  16.9 0.0 copy-done.7
  16.9 17.3 %collective-permute-done = bf16[1,512,1024]{2,1,0:T(8,128)(2,1)S(1)} collective-permute-done((bf16[1,512,1024]{2,1,0:T(8,128)(2,1)}, bf16[1,512,1024]{2,1,0:T(8,128)(2,1)S(1)}, u32[]{:S(2)}, u32[]{:S(2)}) %collective-permute-start) | collective-permute-done | bytes 1048608 | tf_op jit(solution)/shard_map/ppermute | solution.py:10
  34.2 1.6 stack.12
  35.8 0.0 collective-permute-done.1
  35.8 0.8 stack.14
  36.6 8.0 %bitcast_convert_fusion = bf16[2,512,512]{2,0,1:T(2,128)(2,1)} fusion(bf16[1,1,512,2,512]{4,3,0,2,1:T(2,128)(2,1)S(1)} %stack.14, bf16[1,1,512,2,512]{4,3,0,2,1:T(2,128)(2,1)S(1)} %stack.13, bf16[1,1,512,2,512]{4,3,0,2,1:T(2,128)(2,1)} %stack.12, pred[3,2,2]{2,0,1:T(4,128)(4,1)S(1)} %fusion.122), kind=kOutput, calls=%fused_computation.148 | convolution fusion | flops 16252928 | bytes 4194316 | tf_op jit(solution)/shard_map/ksnm,ksimj->snij/dot_general | solution.py:72
  44.6 3.9 convolution_convert_fusion
  48.5 1.6 copy.28
  50.1 0.5 broadcast.323
  50.7 7.0 %reduce = bf16[1024,512]{1,0:T(8,128)(2,1)S(1)} reduce(bf16[1024,1,512]{2,1,0:T(2,128)(2,1)S(1)} %bitcast.173, bf16[]{:T(256)} %broadcast.323), dimensions={1}, to_apply=%bitcast.165.reduce_sub_computation | reduce | bytes 2097154
  57.7 0.8 reshape.317
  58.5 60.3 %all_to_all.36 = bf16[64,2,4096]{2,1,0:T(2,128)(2,1)S(1)} all-to-all(bf16[64,2,4096]{2,1,0:T(2,128)(2,1)S(1)} %reshape.317), channel_id=1, replica_groups=mesh['sec'=8,'xy'=64] {'xy'}, dimensions={0} | all-to-all | bytes 2097152 | tf_op jit(solution)/shard_map/all_to_all | solution.py:85
  118.8 1.0 reshape.318
  119.8 0.3 copy.19
  120.1 0.1 copy.20
  120.2 25.0 %copy.15 = bf16[1,16,32768]{1,0,2:T(2,128)(2,1)} copy(bf16[1,16,32768]{2,1,0:T(8,128)(2,1)S(1)} %bitcast.175) | data formatting | bytes 2097152 | tf_op jit(solution)/shard_map/all_to_all | solution.py:85
  145.2 179.2 %reduce.1 = bf16[32768,16]{1,0:T(8,128)(2,1)} reduce(bf16[32768,1,16]{2,1,0:T(2,128)(2,1)} %bitcast.168, bf16[]{:T(256)} %broadcast.323), dimensions={1}, to_apply=%bitcast.162.reduce_sub_computation | reduce | bytes 2097154
  324.4 10.4 %reshape.319 = bf16[8,2,32768]{2,1,0:T(2,128)(2,1)S(1)} reshape(bf16[32768,16]{1,0:T(8,128)(2,1)} %reduce.1) | data formatting | bytes 2097152
  334.8 25.2 %all_to_all.37 = bf16[8,2,32768]{2,1,0:T(2,128)(2,1)S(1)} all-to-all(bf16[8,2,32768]{2,1,0:T(2,128)(2,1)S(1)} %reshape.319), channel_id=1, replica_groups=mesh['sec'=8,'xy'=64] {'sec'}, dimensions={0} | all-to-all | bytes 2097152 | tf_op jit(solution)/shard_map/all_to_all | solution.py:84
  360.0 12.2 %reshape.320 = bf16[32768,1,16]{2,1,0:T(2,128)(2,1)} reshape(bf16[8,2,32768]{2,1,0:T(2,128)(2,1)S(1)} %all_to_all.37) | data formatting | bytes 2097152
  372.3 29.6 %copy.16 = bf16[1,16,32768]{2,1,0:T(8,128)(2,1)S(1)} copy(bf16[1,16,32768]{1,0,2:T(2,128)(2,1)} %bitcast.169) | data formatting | bytes 2097152 | tf_op jit(solution)/shard_map/all_to_all | solution.py:84
  401.9 0.0 copy-start.5
  402.0 0.6 copy.21
  402.5 0.1 bitcast_bitcast_fusion
  402.6 0.1 fusion.143
  402.7 3.1 collective-permute-start.2
  405.8 1.9 collective-permute-start.3
  407.8 0.7 fusion.146
  408.5 0.0 collective-permute-done.2
  408.5 2.6 collective-permute-done.3
  411.1 1.6 concatenate.13
  412.7 0.0 copy-start
  412.7 3.1 collective-permute-start.4
  415.8 4.6 collective-permute-start.5
  420.4 0.7 fusion.147
  421.1 0.0 collective-permute-done.4
  421.1 0.4 collective-permute-done.5
  421.4 1.4 maximum_convert_fusion
  422.9 0.0 copy-start.6
  422.9 27.6 %fusion.43 = bf16[8,16,4096]{2,0,1:T(8,128)(2,1)} fusion(f32[8,18,4098]{2,0,1:T(8,128)S(1)} %maximum_convert_fusion, f32[]{:T(128)} %bitcast.41, f32[]{:T(128)} %bitcast.40, f32[]{:T(128)} %bitcast.39, f32[]{:T(128)} %bitcast.38, f32[]{:T(128)} %bitcast.37, f32[]{:T(128)} %bitcast.36, f32[]{:T(128)} %bitcast.35, f32[]{:T(128)} %bitcast.34, f32[]{:T(128)} %bitcast.33, ...), kind=kLoop, calls=%fused_computation.80 | loop fusion | flops 28835840 | bytes 22356076 | tf_op jit(solution)/shard_map/convert_element_type | solution.py:102
  450.5 0.9 fusion.142
  451.3 3.0 collective-permute-start.6
  454.3 1.9 collective-permute-start.7
  456.3 0.7 fusion.144
  457.0 0.0 collective-permute-done.6
  457.0 2.6 collective-permute-done.7
  459.6 2.9 concatenate.15
  462.5 0.0 copy-start.1
  462.5 2.3 collective-permute-start.8
  464.8 5.7 %collective-permute-start.9 = (bf16[8,1,4098]{2,0,1:T(8,128)(2,1)S(1)}, bf16[8,1,4098]{2,0,1:T(8,128)(2,1)S(1)}, u32[]{:S(2)}, u32[]{:S(2)}) collective-permute-start(bf16[8,1,4098]{2,0,1:T(8,128)(2,1)S(1)} %get-tuple-element.6), channel_id=1, source_target_pairs={{1,0},{2,1},{3,2},{4,3},{5,4},{6,5},{7,6},{8,7},{9,8},{10,9},{11,1... | collective-permute-start | bytes 196712 | tf_op jit(solution)/shard_map/ppermute | solution.py:21
  470.5 0.7 fusion.145
  471.2 0.0 collective-permute-done.8
  471.2 0.6 collective-permute-done.9
  471.9 1.4 maximum_convert_fusion.1
  473.3 27.6 %fusion.89 = bf16[8,16,4096]{2,0,1:T(8,128)(2,1)} fusion(f32[8,18,4098]{2,0,1:T(8,128)S(1)} %maximum_convert_fusion.1, f32[]{:T(128)} %bitcast.67, f32[]{:T(128)} %bitcast.66, f32[]{:T(128)} %bitcast.65, f32[]{:T(128)} %bitcast.64, f32[]{:T(128)} %bitcast.63, f32[]{:T(128)} %bitcast.62, f32[]{:T(128)} %bitcast.61, f32[]{:T(128)} %bitcast.60, f32[]{:T(128)} %bitcast.59, ...), kind=kLoop, calls=%fused_computation.126 | loop fusion | flops 29360128 | bytes 23404652 | tf_op jit(solution)/shard_map/convert_element_type | solution.py:107
  500.9 2.8 copy.17
  (16 shorter events, 0.1 us)
Async XLA Ops:
  0.0 16.8 %copy-start.8 = (s32[1,2,2]{2,1,0:T(2,128)S(1)}, s32[1,2,2]{2,1,0:T(2,128)}, u32[]{:S(2)}) copy-start(s32[1,2,2]{2,1,0:T(2,128)} %param.6) | copy-start | bytes 52
  0.0 16.9 %copy-start.7 = (f32[1,2,2]{2,1,0:T(2,128)S(1)}, f32[1,2,2]{2,1,0:T(2,128)}, u32[]{:S(2)}) copy-start(f32[1,2,2]{2,1,0:T(2,128)} %param.7) | copy-start | bytes 52
  0.0 34.2 %collective-permute-start = (bf16[1,512,1024]{2,1,0:T(8,128)(2,1)}, bf16[1,512,1024]{2,1,0:T(8,128)(2,1)S(1)}, u32[]{:S(2)}, u32[]{:S(2)}) collective-permute-start(bf16[1,512,1024]{2,1,0:T(8,128)(2,1)} %param.5), channel_id=1, source_target_pairs={{0,1},{1,2},{2,3},{3,4},{4,5},{5,6},{6,7},{7,8},{8,9},{9,10},{10,1... | collective-permute-start | bytes 3145736 | tf_op jit(solution)/shard_map/ppermute | solution.py:10
  3.7 32.1 %collective-permute-start.1 = (bf16[1,512,1024]{2,1,0:T(8,128)(2,1)}, bf16[1,512,1024]{2,1,0:T(8,128)(2,1)S(1)}, u32[]{:S(2)}, u32[]{:S(2)}) collective-permute-start(bf16[1,512,1024]{2,1,0:T(8,128)(2,1)} %param.5), channel_id=1, source_target_pairs={{1,0},{2,1},{3,2},{4,3},{5,4},{6,5},{7,6},{8,7},{9,8},{10,9},{11,1... | collective-permute-start | bytes 3145736 | tf_op jit(solution)/shard_map/ppermute | solution.py:10
  36.6 8.0 %copy-start.2 = (pred[512,512]{1,0:T(8,128)(4,1)S(1)}, pred[512,512]{1,0:T(8,128)(4,1)}, u32[]{:S(2)}) copy-start(pred[512,512]{1,0:T(8,128)(4,1)} %get-tuple-element.78) | copy-start | bytes 786436
  36.6 8.0 %copy-start.3 = (pred[512,512]{1,0:T(8,128)(4,1)S(1)}, pred[512,512]{1,0:T(8,128)(4,1)}, u32[]{:S(2)}) copy-start(pred[512,512]{1,0:T(8,128)(4,1)} %get-tuple-element.79) | copy-start | bytes 786436
  36.6 8.0 %copy-start.4 = (pred[512,512]{1,0:T(8,128)(4,1)S(1)}, pred[512,512]{1,0:T(8,128)(4,1)}, u32[]{:S(2)}) copy-start(pred[512,512]{1,0:T(8,128)(4,1)} %get-tuple-element.80) | copy-start | bytes 786436
  401.9 5.8 %copy-start.5 = (f32[3,3,3]{2,1,0:T(4,128)S(1)}, f32[3,3,3]{2,1,0:T(4,128)}, u32[]{:S(2)}) copy-start(f32[3,3,3]{2,1,0:T(4,128)} %param.8) | copy-start | bytes 328
  402.7 5.8 %collective-permute-start.2 = (bf16[8,16,1]{2,0,1:T(8,128)(2,1)S(1)}, bf16[8,16,1]{2,0,1:T(8,128)(2,1)S(1)}, u32[]{:S(2)}, u32[]{:S(2)}) collective-permute-start(bf16[8,16,1]{2,0,1:T(8,128)(2,1)S(1)} %get-tuple-element.12), channel_id=1, source_target_pairs={{0,64},{64,128},{128,192},{192,256},{256,320},{320,384},{384,448},... | collective-permute-start | bytes 776 | tf_op jit(solution)/shard_map/ppermute | solution.py:20
  405.8 5.2 %collective-permute-start.3 = (bf16[8,16,1]{2,0,1:T(8,128)(2,1)S(1)}, bf16[8,16,1]{2,0,1:T(8,128)(2,1)S(1)}, u32[]{:S(2)}, u32[]{:S(2)}) collective-permute-start(bf16[8,16,1]{2,0,1:T(8,128)(2,1)S(1)} %get-tuple-element.11), channel_id=1, source_target_pairs={{64,0},{128,64},{192,128},{256,192},{320,256},{384,320},{448,384},... | collective-permute-start | bytes 776 | tf_op jit(solution)/shard_map/ppermute | solution.py:21
  412.7 8.4 %copy-start = (bf16[8,16,4098]{2,0,1:T(8,128)(2,1)}, bf16[8,16,4098]{2,0,1:T(8,128)(2,1)S(1)}, u32[]{:S(2)}) copy-start(bf16[8,16,4098]{2,0,1:T(8,128)(2,1)S(1)} %concatenate.13) | copy-start | bytes 3147268
  412.7 8.4 %collective-permute-start.4 = (bf16[8,1,4098]{2,0,1:T(8,128)(2,1)S(1)}, bf16[8,1,4098]{2,0,1:T(8,128)(2,1)S(1)}, u32[]{:S(2)}, u32[]{:S(2)}) collective-permute-start(bf16[8,1,4098]{2,0,1:T(8,128)(2,1)S(1)} %get-tuple-element.7), channel_id=1, source_target_pairs={{0,1},{1,2},{2,3},{3,4},{4,5},{5,6},{6,7},{7,8},{8,9},{9,10},{10,1... | collective-permute-start | bytes 196712 | tf_op jit(solution)/shard_map/ppermute | solution.py:20
  415.8 5.7 %collective-permute-start.5 = (bf16[8,1,4098]{2,0,1:T(8,128)(2,1)S(1)}, bf16[8,1,4098]{2,0,1:T(8,128)(2,1)S(1)}, u32[]{:S(2)}, u32[]{:S(2)}) collective-permute-start(bf16[8,1,4098]{2,0,1:T(8,128)(2,1)S(1)} %get-tuple-element.8), channel_id=1, source_target_pairs={{1,0},{2,1},{3,2},{4,3},{5,4},{6,5},{7,6},{8,7},{9,8},{10,9},{11,1... | collective-permute-start | bytes 196712 | tf_op jit(solution)/shard_map/ppermute | solution.py:21
  422.9 33.4 %copy-start.6 = (f32[3,3,3]{2,1,0:T(4,128)S(1)}, f32[3,3,3]{2,1,0:T(4,128)}, u32[]{:S(2)}) copy-start(f32[3,3,3]{2,1,0:T(4,128)} %param.9) | copy-start | bytes 328
  451.3 5.7 %collective-permute-start.6 = (bf16[8,16,1]{2,0,1:T(8,128)(2,1)S(1)}, bf16[8,16,1]{2,0,1:T(8,128)(2,1)S(1)}, u32[]{:S(2)}, u32[]{:S(2)}) collective-permute-start(bf16[8,16,1]{2,0,1:T(8,128)(2,1)S(1)} %get-tuple-element.10), channel_id=1, source_target_pairs={{0,64},{64,128},{128,192},{192,256},{256,320},{320,384},{384,448},... | collective-permute-start | bytes 776 | tf_op jit(solution)/shard_map/ppermute | solution.py:20
  454.3 5.2 %collective-permute-start.7 = (bf16[8,16,1]{2,0,1:T(8,128)(2,1)S(1)}, bf16[8,16,1]{2,0,1:T(8,128)(2,1)S(1)}, u32[]{:S(2)}, u32[]{:S(2)}) collective-permute-start(bf16[8,16,1]{2,0,1:T(8,128)(2,1)S(1)} %get-tuple-element.9), channel_id=1, source_target_pairs={{64,0},{128,64},{192,128},{256,192},{320,256},{384,320},{448,384},... | collective-permute-start | bytes 776 | tf_op jit(solution)/shard_map/ppermute | solution.py:21
  462.5 8.7 %copy-start.1 = (bf16[8,16,4098]{2,0,1:T(8,128)(2,1)}, bf16[8,16,4098]{2,0,1:T(8,128)(2,1)S(1)}, u32[]{:S(2)}) copy-start(bf16[8,16,4098]{2,0,1:T(8,128)(2,1)S(1)} %concatenate.15) | copy-start | bytes 3147268
  462.5 8.7 %collective-permute-start.8 = (bf16[8,1,4098]{2,0,1:T(8,128)(2,1)S(1)}, bf16[8,1,4098]{2,0,1:T(8,128)(2,1)S(1)}, u32[]{:S(2)}, u32[]{:S(2)}) collective-permute-start(bf16[8,1,4098]{2,0,1:T(8,128)(2,1)S(1)} %get-tuple-element.5), channel_id=1, source_target_pairs={{0,1},{1,2},{2,3},{3,4},{4,5},{5,6},{6,7},{7,8},{8,9},{9,10},{10,1... | collective-permute-start | bytes 196712 | tf_op jit(solution)/shard_map/ppermute | solution.py:20
  464.8 7.0 %collective-permute-start.9 = (bf16[8,1,4098]{2,0,1:T(8,128)(2,1)S(1)}, bf16[8,1,4098]{2,0,1:T(8,128)(2,1)S(1)}, u32[]{:S(2)}, u32[]{:S(2)}) collective-permute-start(bf16[8,1,4098]{2,0,1:T(8,128)(2,1)S(1)} %get-tuple-element.6), channel_id=1, source_target_pairs={{1,0},{2,1},{3,2},{4,3},{5,4},{6,5},{7,6},{8,7},{9,8},{10,9},{11,1... | collective-permute-start | bytes 196712 | tf_op jit(solution)/shard_map/ppermute | solution.py:21
where the time goes:
time: 506 us; the launch traced here: 504 us
  other arithmetic  246 us (49%)
  local copies, waits for them, and re-layouts  97.5 us (19%)
  blocking collectives  85.5 us (17%)
  starting transfers between devices  38.7 us (8%)
  waiting for transfers between devices  23.4 us (5%)
  matrix products  11.9 us (2%)
    unnamed x2, other arithmetic  186 us
    all_to_all x1, blocking collectives, body(): lax.all_to_all(aligned_strip, 'xy', split_axis=1, concat_axis=2, tiled=True)  60.3 us
    all_to_all x2, local copies, waits for them, and re-layouts, body(): lax.all_to_all(lax.all_to_all(aligned_strip, 'xy', split_axis=1, concat_a...  29.7 us
    convert_element_type x1, other arithmetic, body(): return (second + group_data.astype(jnp.float32)).astype(jnp.bfloat16)  27.6 us
    convert_element_type x1, other arithmetic, body(): first_pass = jnp.maximum(stencil(pad_sections(rim_one.astype(jnp.float32)...  27.6 us
    unnamed x25, local copies, waits for them, and re-layouts  25.9 us
    all_to_all x1, blocking collectives, body(): lax.all_to_all(lax.all_to_all(aligned_strip, 'xy', split_axis=1, concat_a...  25.2 us
    all_to_all x2, local copies, waits for them, and re-layouts, body(): lax.all_to_all(aligned_strip, 'xy', split_axis=1, concat_axis=2, tiled=True)  25.1 us
  transfers between devices with their start and end apart: 10, of which 5 were waited for; matrix products, arithmetic and copies ran while one was open for 2% of the time, Pallas kernels for 0%

commit v1 on v0

--- a/solution.py
+++ b/solution.py
@@ -2,6 +2,29 @@
 import jax.numpy as jnp
 from jax import lax
 from jax.sharding import PartitionSpec as P
+
+
+def in_blocks(x, dim, count):
+    dims = x.shape
+    blocks = x.reshape(*dims[:dim], count, dims[dim] // count, *dims[dim + 1 :])
+    return jnp.moveaxis(blocks, dim, 0)
+
+
+def laid_out(blocks, dim):
+    blocks = jnp.moveaxis(blocks, 0, dim)
+    shape = blocks.shape
+    return blocks.reshape(*shape[:dim], shape[dim] * shape[dim + 1], *shape[dim + 2 :])
+
+
+def swapped_with_each(x, axis, split_dim, concat_dim):
+    peers, position = (lax.axis_size(axis), lax.axis_index(axis))
+    blocks = in_blocks(x, split_dim, peers)
+    outs = [blocks[position]]
+    for step in range(1, peers):
+        sent = blocks[position ^ step]
+        outs.append(lax.ppermute(sent, axis, [(i, i ^ step) for i in range(peers)]))
+    blocks = jnp.stack(outs)[position ^ jnp.arange(peers)]
+    return laid_out(blocks, concat_dim)
 
 
 def from_behind(value, axis, steps):
@@ -81,12 +104,8 @@
         "sncj,snrj->sncr", col_matrix, rows_warped, preferred_element_type=jnp.float32
     ).astype(jnp.bfloat16)
     aligned_strip = warped.reshape(sections_dev, width, edge)
-    group_data = lax.all_to_all(
-        lax.all_to_all(aligned_strip, "xy", split_axis=1, concat_axis=2, tiled=True),
-        "sec",
-        split_axis=2,
-        concat_axis=0,
-        tiled=True,
+    group_data = swapped_with_each(
+        lax.all_to_all(aligned_strip, "xy", split_axis=1, concat_axis=2, tiled=True), "sec", 2, 0
     )
     sections_all, group_cols, group_rows = group_data.shape
     rim_one = with_halo(group_data, (("sec", 2), ("xy", 1)), 1)

time: 506 us -> 258 us (0.51)
  other arithmetic: 246 us -> 64.7 us
  blocking collectives: 85.5 us -> 0 us
  local copies, waits for them, and re-layouts: 97.5 us -> 21.8 us
  waiting for transfers between devices: 23.4 us -> 78.4 us
  starting transfers between devices: 38.7 us -> 79.6 us
    unnamed x2 -> x1, other arithmetic: 186 us -> 7.04 us
    all_to_all x2 -> x0, blocking collectives: 85.5 us -> none  [the longest x1 60.3 us: body(): lax.all_to_all(aligned_strip, 'xy', split_axis=1, concat_axis=2, tiled=True)]
    all_to_all x0 -> x1, waiting for transfers between devices: none -> 48.7 us  [body(): lax.all_to_all(aligned_strip, 'xy', split_axis=1, concat_axis=2, tiled=True)]
    all_to_all x2 -> x0, local copies, waits for them, and re-layouts: 29.7 us -> none  [body(): lax.all_to_all(lax.all_to_all(aligned_strip, 'xy', split_axis=1, concat_a...]
    ppermute x0 -> x7, starting transfers between devices: none -> 27.3 us  [swapped_with_each(): outs.append(lax.ppermute(sent, axis, [(i, i ^ step) for i in range(peers)]))]
    all_to_all x2 -> x1, local copies, waits for them, and re-layouts: 25.1 us -> 0.58 us  [body(): lax.all_to_all(aligned_strip, 'xy', split_axis=1, concat_axis=2, tiled=True)]
    unnamed x25 -> x28, local copies, waits for them, and re-layouts: 25.9 us -> 4.72 us
    all_to_all x0 -> x1, starting transfers between devices: none -> 11.7 us  [body(): lax.all_to_all(aligned_strip, 'xy', split_axis=1, concat_axis=2, tiled=True)]
  transfers between devices with their start and end apart: 10 -> 18, of which waited for: 5 -> 9; matrix products, arithmetic and copies ran while one was open for 2% -> 4% of each run, Pallas kernels for 0% -> 0%
where the time goes in v1:
time: 258 us; the launch traced here: 257 us
  starting transfers between devices  79.6 us (31%)
  waiting for transfers between devices  78.4 us (30%)
  other arithmetic  64.7 us (25%)
  local copies, waits for them, and re-layouts  21.8 us (8%)
  matrix products  12.3 us (5%)
    all_to_all x1, waiting for transfers between devices, body(): lax.all_to_all(aligned_strip, 'xy', split_axis=1, concat_axis=2, tiled=True)  48.7 us
    convert_element_type x1, other arithmetic, body(): return (second + group_data.astype(jnp.float32)).astype(jnp.bfloat16)  27.6 us
    ppermute x7, starting transfers between devices, swapped_with_each(): outs.append(lax.ppermute(sent, axis, [(i, i ^ step) for i in range(peers)]))  27.3 us
    convert_element_type x1, other arithmetic, body(): first_pass = jnp.maximum(stencil(pad_sections(rim_one.astype(jnp.float32)...  26.9 us
    ppermute x2, waiting for transfers between devices, from_behind(): lax.ppermute(value, axis, [(source, source + steps) for source in range(f...  17.3 us
    ppermute x4, starting transfers between devices, with_halo(): after = lax.ppermute(first, axis, down)  14.5 us
    ppermute x2, starting transfers between devices, from_behind(): lax.ppermute(value, axis, [(source, source + steps) for source in range(f...  13.1 us
    ppermute x4, starting transfers between devices, with_halo(): before = lax.ppermute(last, axis, up)  12.9 us
  transfers between devices with their start and end apart: 18, of which 9 were waited for; matrix products, arithmetic and copies ran while one was open for 4% of the time, Pallas kernels for 0%

profile of v1, /device:TPU:9, one launch (start us, length us, event | category | flops | bytes accessed | tf_op | source)
XLA Modules:
  0.0 257.3 jit_solution(12826079727294997189)
XLA Ops:
  0.0 3.7 %collective-permute-start = (bf16[1,512,1024]{2,1,0:T(8,128)(2,1)}, bf16[1,512,1024]{2,1,0:T(8,128)(2,1)S(1)}, u32[]{:S(2)}, u32[]{:S(2)}) collective-permute-start(bf16[1,512,1024]{2,1,0:T(8,128)(2,1)} %param.5), channel_id=1, source_target_pairs={{0,1},{1,2},{2,3},{3,4},{4,5},{5,6},{6,7},{7,8},{8,9},{9,10},{10,1... | collective-permute-start | bytes 3145736 | tf_op jit(solution)/shard_map/ppermute | solution.py:33
  3.7 9.4 %collective-permute-start.1 = (bf16[1,512,1024]{2,1,0:T(8,128)(2,1)}, bf16[1,512,1024]{2,1,0:T(8,128)(2,1)S(1)}, u32[]{:S(2)}, u32[]{:S(2)}) collective-permute-start(bf16[1,512,1024]{2,1,0:T(8,128)(2,1)} %param.5), channel_id=1, source_target_pairs={{1,0},{2,1},{3,2},{4,3},{5,4},{6,5},{7,6},{8,7},{9,8},{10,9},{11,1... | collective-permute-start | bytes 3145736 | tf_op jit(solution)/shard_map/ppermute | solution.py:33
  13.1 0.9 fusion.109
  13.9 1.8 stack.37
  15.8 1.0 fusion.111
  17.0 17.3 %collective-permute-done = bf16[1,512,1024]{2,1,0:T(8,128)(2,1)S(1)} collective-permute-done((bf16[1,512,1024]{2,1,0:T(8,128)(2,1)}, bf16[1,512,1024]{2,1,0:T(8,128)(2,1)S(1)}, u32[]{:S(2)}, u32[]{:S(2)}) %collective-permute-start) | collective-permute-done | bytes 1048608 | tf_op jit(solution)/shard_map/ppermute | solution.py:33
  34.2 1.6 stack.36
  35.8 1.6 stack.38
  37.4 7.9 %bitcast_convert_fusion = bf16[2,512,512]{2,0,1:T(2,128)(2,1)} fusion(bf16[1,1,512,2,512]{4,3,0,2,1:T(2,128)(2,1)} %stack.38, bf16[1,1,512,2,512]{4,3,0,2,1:T(2,128)(2,1)S(1)} %stack.37, bf16[1,1,512,2,512]{4,3,0,2,1:T(2,128)(2,1)S(1)} %copy-done, pred[3,2,2]{2,0,1:T(4,128)(4,1)S(1)} %fusion.122), kind=kOutput, calls=%fused_computation.149 | convolution fusion | flops 16252928 | bytes 4194316 | tf_op jit(solution)/shard_map/ksnm,ksimj->snij/dot_general | solution.py:95
  45.3 4.4 %convolution_convert_fusion = bf16[2,512,512]{2,1,0:T(8,128)(2,1)S(1)} fusion(bf16[2,512,512]{2,0,1:T(2,128)(2,1)} %bitcast_convert_fusion, f32[2]{0:T(128)S(1)} %get-tuple-element.79, f32[2]{0:T(128)S(1)} %get-tuple-element.80, f32[2]{0:T(128)S(1)} %get-tuple-element.81, f32[2]{0:T(128)S(1)} %get-tuple-element.82, f32[2]{0:T(128)S(1)} %get-tuple-element.76, ...), kind=kOutput, calls=%fused_computation.154 | convolution fusion | flops 1083179008 | bytes 3145792 | tf_op jit(solution)/shard_map/sncj,snrj->sncr/dot_general | solution.py:103
  49.7 1.6 copy.47
  51.3 0.5 broadcast.358
  51.8 7.0 %reduce = bf16[1024,512]{1,0:T(8,128)(2,1)S(1)} reduce(bf16[1024,1,512]{2,1,0:T(2,128)(2,1)S(1)} %bitcast.194, bf16[]{:T(256)} %broadcast.358), dimensions={1}, to_apply=%bitcast.192.reduce_sub_computation | reduce | bytes 2097154
  58.9 1.6 reshape.368
  60.4 11.7 %all-to-all-start = ((bf16[64,2,4096]{2,1,0:T(2,128)(2,1)}), bf16[64,2,4096]{2,1,0:T(2,128)(2,1)S(1)}, u32[]{:S(2)}, u32[]{:S(2)}) async-start(bf16[64,2,4096]{2,1,0:T(2,128)(2,1)} %reshape.368), calls=%async_computation | async-start | bytes 2097152 | tf_op jit(solution)/shard_map/all_to_all | solution.py:108
  72.2 48.7 %all-to-all-done = bf16[64,2,4096]{2,1,0:T(2,128)(2,1)S(1)} async-done(((bf16[64,2,4096]{2,1,0:T(2,128)(2,1)}), bf16[64,2,4096]{2,1,0:T(2,128)(2,1)S(1)}, u32[]{:S(2)}, u32[]{:S(2)}) %all-to-all-start) | async-done | bytes 1048608 | tf_op jit(solution)/shard_map/all_to_all | solution.py:108
  120.9 1.0 reshape.369
  122.0 0.3 copy.17
  122.3 0.6 copy.14
  122.9 0.5 reshape.353
  123.4 2.3 constant_dynamic-slice_fusion
  125.7 0.2 copy.46
  125.8 8.0 %collective-permute-start.2 = (bf16[1,16,4096]{2,1,0:T(8,128)(2,1)S(1)}, bf16[1,16,4096]{2,1,0:T(8,128)(2,1)S(1)}, u32[]{:S(2)}, u32[]{:S(2)}) collective-permute-start(bf16[1,16,4096]{2,1,0:T(8,128)(2,1)S(1)} %bitcast.204), channel_id=1, source_target_pairs={{0,64},{64,0},{128,192},{192,128},{256,320},{320,256},{384,448},{4... | collective-permute-start | bytes 393224 | tf_op jit(solution)/shard_map/ppermute | solution.py:25
  133.8 0.2 bitcast_dynamic-update-slice_fusion
  134.0 0.2 copy.45
  134.2 3.1 %collective-permute-start.3 = (bf16[1,16,4096]{2,1,0:T(8,128)(2,1)S(1)}, bf16[1,16,4096]{2,1,0:T(8,128)(2,1)S(1)}, u32[]{:S(2)}, u32[]{:S(2)}) collective-permute-start(bf16[1,16,4096]{2,1,0:T(8,128)(2,1)S(1)} %bitcast.203), channel_id=1, source_target_pairs={{0,128},{64,192},{128,0},{192,64},{256,384},{320,448},{384,256},{4... | collective-permute-start | bytes 393224 | tf_op jit(solution)/shard_map/ppermute | solution.py:25
  137.3 0.2 copy.44
  137.4 2.3 collective-permute-start.4
  139.8 0.2 copy.43
  139.9 4.7 %collective-permute-start.5 = (bf16[1,16,4096]{2,1,0:T(8,128)(2,1)S(1)}, bf16[1,16,4096]{2,1,0:T(8,128)(2,1)S(1)}, u32[]{:S(2)}, u32[]{:S(2)}) collective-permute-start(bf16[1,16,4096]{2,1,0:T(8,128)(2,1)S(1)} %bitcast.201), channel_id=1, source_target_pairs={{0,256},{64,320},{128,384},{192,448},{256,0},{320,64},{384,128},{4... | collective-permute-start | bytes 393224 | tf_op jit(solution)/shard_map/ppermute | solution.py:25
  144.6 0.2 copy.42
  144.8 2.5 collective-permute-start.6
  147.3 0.2 copy.41
  147.4 0.2 copy.40
  147.6 4.4 %collective-permute-start.7 = (bf16[1,16,4096]{2,1,0:T(8,128)(2,1)S(1)}, bf16[1,16,4096]{2,1,0:T(8,128)(2,1)S(1)}, u32[]{:S(2)}, u32[]{:S(2)}) collective-permute-start(bf16[1,16,4096]{2,1,0:T(8,128)(2,1)S(1)} %bitcast.199), channel_id=1, source_target_pairs={{0,384},{64,448},{128,256},{192,320},{256,128},{320,192},{384,0},{... | collective-permute-start | bytes 393224 | tf_op jit(solution)/shard_map/ppermute | solution.py:25
  152.1 2.3 collective-permute-start.8
  154.4 2.4 collective-permute-done.7
  156.9 3.7 %collective-permute-done.8 = bf16[1,16,4096]{2,1,0:T(8,128)(2,1)S(1)} collective-permute-done((bf16[1,16,4096]{2,1,0:T(8,128)(2,1)S(1)}, bf16[1,16,4096]{2,1,0:T(8,128)(2,1)S(1)}, u32[]{:S(2)}, u32[]{:S(2)}) %collective-permute-start.8) | collective-permute-done | bytes 131104 | tf_op jit(solution)/shard_map/ppermute | solution.py:25
  160.6 0.6 gather_fusion
  161.3 2.3 collective-permute-start.10
  163.6 3.3 %collective-permute-start.9 = (bf16[8,16,1]{2,1,0:T(8,128)(2,1)S(1)}, bf16[8,16,1]{2,1,0:T(8,128)(2,1)S(1)}, u32[]{:S(2)}, u32[]{:S(2)}) collective-permute-start(bf16[8,16,1]{2,1,0:T(8,128)(2,1)S(1)} %get-tuple-element.12), channel_id=1, source_target_pairs={{0,64},{64,128},{128,192},{192,256},{256,320},{320,384},{384,448},... | collective-permute-start | bytes 776 | tf_op jit(solution)/shard_map/ppermute | solution.py:43
  166.9 0.7 fusion.147
  167.6 0.3 collective-permute-done.9
  167.9 1.6 concatenate.13
  169.4 0.2 fusion.142
  169.7 3.0 %collective-permute-start.11 = (bf16[8,1,4098]{2,1,0:T(2,128)(2,1)S(1)}, bf16[8,1,4098]{2,1,0:T(2,128)(2,1)S(1)}, u32[]{:S(2)}, u32[]{:S(2)}) collective-permute-start(bf16[8,1,4098]{2,1,0:T(2,128)(2,1)S(1)} %get-tuple-element.7), channel_id=1, source_target_pairs={{0,1},{1,2},{2,3},{3,4},{4,5},{5,6},{6,7},{7,8},{8,9},{9,10},{10,1... | collective-permute-start | bytes 196712 | tf_op jit(solution)/shard_map/ppermute | solution.py:43
  172.7 4.3 %collective-permute-start.12 = (bf16[8,1,4098]{2,1,0:T(2,128)(2,1)S(1)}, bf16[8,1,4098]{2,1,0:T(2,128)(2,1)S(1)}, u32[]{:S(2)}, u32[]{:S(2)}) collective-permute-start(bf16[8,1,4098]{2,1,0:T(2,128)(2,1)S(1)} %get-tuple-element.8), channel_id=1, source_target_pairs={{1,0},{2,1},{3,2},{4,3},{5,4},{6,5},{7,6},{8,7},{9,8},{10,9},{11,1... | collective-permute-start | bytes 196712 | tf_op jit(solution)/shard_map/ppermute | solution.py:44
  177.1 0.7 fusion.148
  177.7 0.7 collective-permute-done.11
  178.4 1.8 collective-permute-done.12
  180.2 0.6 maximum_convert_fusion
  180.8 26.9 %fusion.43 = bf16[8,16,4096]{2,1,0:T(8,128)(2,1)S(1)} fusion(f32[8,18,4098]{2,1,0:T(8,128)S(1)} %maximum_convert_fusion, f32[]{:T(128)} %bitcast.48, f32[]{:T(128)} %bitcast.47, f32[]{:T(128)} %bitcast.46, f32[]{:T(128)} %bitcast.45, f32[]{:T(128)} %bitcast.44, f32[]{:T(128)} %bitcast.43, f32[]{:T(128)} %bitcast.42, f32[]{:T(128)} %bitcast.41, f32[]{:T(128)} %bitcast.40, ...), kind=kLoop, calls=%fused_computation.81 | loop fusion | flops 28835840 | bytes 23167084 | tf_op jit(solution)/shard_map/convert_element_type | solution.py:121
  207.7 4.2 %collective-permute-start.13 = (bf16[8,16,1]{2,1,0:T(8,128)(2,1)S(1)}, bf16[8,16,1]{2,1,0:T(8,128)(2,1)S(1)}, u32[]{:S(2)}, u32[]{:S(2)}) collective-permute-start(bf16[8,16,1]{2,1,0:T(8,128)(2,1)S(1)} %get-tuple-element.10), channel_id=1, source_target_pairs={{0,64},{64,128},{128,192},{192,256},{256,320},{320,384},{384,448},... | collective-permute-start | bytes 776 | tf_op jit(solution)/shard_map/ppermute | solution.py:43
  212.0 1.9 collective-permute-start.14
  213.9 0.7 fusion.145
  214.6 2.6 %collective-permute-done.14 = bf16[8,16,1]{2,1,0:T(8,128)(2,1)S(1)} collective-permute-done((bf16[8,16,1]{2,1,0:T(8,128)(2,1)S(1)}, bf16[8,16,1]{2,1,0:T(8,128)(2,1)S(1)}, u32[]{:S(2)}, u32[]{:S(2)}) %collective-permute-start.14) | collective-permute-done | bytes 288 | tf_op jit(solution)/shard_map/ppermute | solution.py:44
  217.2 1.6 concatenate.15
  218.8 0.2 fusion.141
  219.0 2.4 collective-permute-start.15
  221.4 6.0 %collective-permute-start.16 = (bf16[8,1,4098]{2,1,0:T(2,128)(2,1)S(1)}, bf16[8,1,4098]{2,1,0:T(2,128)(2,1)S(1)}, u32[]{:S(2)}, u32[]{:S(2)}) collective-permute-start(bf16[8,1,4098]{2,1,0:T(2,128)(2,1)S(1)} %get-tuple-element.6), channel_id=1, source_target_pairs={{1,0},{2,1},{3,2},{4,3},{5,4},{6,5},{7,6},{8,7},{9,8},{10,9},{11,1... | collective-permute-start | bytes 196712 | tf_op jit(solution)/shard_map/ppermute | solution.py:44
  227.4 0.7 fusion.146
  228.1 1.0 collective-permute-done.16
  229.1 0.6 maximum_convert_fusion.1
  229.7 27.6 %fusion.89 = bf16[8,16,4096]{2,1,0:T(8,128)(2,1)} fusion(f32[8,18,4098]{2,1,0:T(8,128)S(1)} %maximum_convert_fusion.1, bf16[8,16,4096]{2,1,0:T(8,128)(2,1)S(1)} %gather_fusion, f32[]{:T(128)} %bitcast.74, f32[]{:T(128)} %bitcast.73, f32[]{:T(128)} %bitcast.72, f32[]{:T(128)} %bitcast.71, f32[]{:T(128)} %bitcast.70, f32[]{:T(128)} %bitcast.69, f32[]{:T(128)} %bitcast.68, ...), kind=kLoop, calls=%fused_computation.127 | loop fusion | flops 29360128 | bytes 24215660 | tf_op jit(solution)/shard_map/convert_element_type | solution.py:126
  (34 shorter events, 0.5 us)
Async XLA Ops:
  0.0 16.8 %copy-start.4 = (s32[1,2,2]{2,1,0:T(2,128)S(1)}, s32[1,2,2]{2,1,0:T(2,128)}, u32[]{:S(2)}) copy-start(s32[1,2,2]{2,1,0:T(2,128)} %param.6) | copy-start | bytes 52
  0.0 16.9 %copy-start.3 = (f32[1,2,2]{2,1,0:T(2,128)S(1)}, f32[1,2,2]{2,1,0:T(2,128)}, u32[]{:S(2)}) copy-start(f32[1,2,2]{2,1,0:T(2,128)} %param.7) | copy-start | bytes 52
  0.0 34.2 %collective-permute-start = (bf16[1,512,1024]{2,1,0:T(8,128)(2,1)}, bf16[1,512,1024]{2,1,0:T(8,128)(2,1)S(1)}, u32[]{:S(2)}, u32[]{:S(2)}) collective-permute-start(bf16[1,512,1024]{2,1,0:T(8,128)(2,1)} %param.5), channel_id=1, source_target_pairs={{0,1},{1,2},{2,3},{3,4},{4,5},{5,6},{6,7},{7,8},{8,9},{9,10},{10,1... | collective-permute-start | bytes 3145736 | tf_op jit(solution)/shard_map/ppermute | solution.py:33
  3.7 32.1 %collective-permute-start.1 = (bf16[1,512,1024]{2,1,0:T(8,128)(2,1)}, bf16[1,512,1024]{2,1,0:T(8,128)(2,1)S(1)}, u32[]{:S(2)}, u32[]{:S(2)}) collective-permute-start(bf16[1,512,1024]{2,1,0:T(8,128)(2,1)} %param.5), channel_id=1, source_target_pairs={{1,0},{2,1},{3,2},{4,3},{5,4},{6,5},{7,6},{8,7},{9,8},{10,9},{11,1... | collective-permute-start | bytes 3145736 | tf_op jit(solution)/shard_map/ppermute | solution.py:33
  35.8 1.6 copy-start
  60.4 60.5 %all-to-all-start = ((bf16[64,2,4096]{2,1,0:T(2,128)(2,1)}), bf16[64,2,4096]{2,1,0:T(2,128)(2,1)S(1)}, u32[]{:S(2)}, u32[]{:S(2)}) async-start(bf16[64,2,4096]{2,1,0:T(2,128)(2,1)} %reshape.368), calls=%async_computation | async-start | bytes 2097152 | tf_op jit(solution)/shard_map/all_to_all | solution.py:108
  125.8 21.8 %collective-permute-start.2 = (bf16[1,16,4096]{2,1,0:T(8,128)(2,1)S(1)}, bf16[1,16,4096]{2,1,0:T(8,128)(2,1)S(1)}, u32[]{:S(2)}, u32[]{:S(2)}) collective-permute-start(bf16[1,16,4096]{2,1,0:T(8,128)(2,1)S(1)} %bitcast.204), channel_id=1, source_target_pairs={{0,64},{64,0},{128,192},{192,128},{256,320},{320,256},{384,448},{4... | collective-permute-start | bytes 393224 | tf_op jit(solution)/shard_map/ppermute | solution.py:25
  134.2 17.9 %collective-permute-start.3 = (bf16[1,16,4096]{2,1,0:T(8,128)(2,1)S(1)}, bf16[1,16,4096]{2,1,0:T(8,128)(2,1)S(1)}, u32[]{:S(2)}, u32[]{:S(2)}) collective-permute-start(bf16[1,16,4096]{2,1,0:T(8,128)(2,1)S(1)} %bitcast.203), channel_id=1, source_target_pairs={{0,128},{64,192},{128,0},{192,64},{256,384},{320,448},{384,256},{4... | collective-permute-start | bytes 393224 | tf_op jit(solution)/shard_map/ppermute | solution.py:25
  137.4 16.9 %collective-permute-start.4 = (bf16[1,16,4096]{2,1,0:T(8,128)(2,1)S(1)}, bf16[1,16,4096]{2,1,0:T(8,128)(2,1)S(1)}, u32[]{:S(2)}, u32[]{:S(2)}) collective-permute-start(bf16[1,16,4096]{2,1,0:T(8,128)(2,1)S(1)} %bitcast.202), channel_id=1, source_target_pairs={{0,192},{64,128},{128,64},{192,0},{256,448},{320,384},{384,320},{4... | collective-permute-start | bytes 393224 | tf_op jit(solution)/shard_map/ppermute | solution.py:25
  139.9 14.4 %collective-permute-start.5 = (bf16[1,16,4096]{2,1,0:T(8,128)(2,1)S(1)}, bf16[1,16,4096]{2,1,0:T(8,128)(2,1)S(1)}, u32[]{:S(2)}, u32[]{:S(2)}) collective-permute-start(bf16[1,16,4096]{2,1,0:T(8,128)(2,1)S(1)} %bitcast.201), channel_id=1, source_target_pairs={{0,256},{64,320},{128,384},{192,448},{256,0},{320,64},{384,128},{4... | collective-permute-start | bytes 393224 | tf_op jit(solution)/shard_map/ppermute | solution.py:25
  144.8 9.6 %collective-permute-start.6 = (bf16[1,16,4096]{2,1,0:T(8,128)(2,1)S(1)}, bf16[1,16,4096]{2,1,0:T(8,128)(2,1)S(1)}, u32[]{:S(2)}, u32[]{:S(2)}) collective-permute-start(bf16[1,16,4096]{2,1,0:T(8,128)(2,1)S(1)} %bitcast.200), channel_id=1, source_target_pairs={{0,320},{64,256},{128,448},{192,384},{256,64},{320,0},{384,192},{4... | collective-permute-start | bytes 393224 | tf_op jit(solution)/shard_map/ppermute | solution.py:25
  147.6 19.3 %copy-start.1 = (f32[3,3,3]{2,1,0:T(4,128)S(1)}, f32[3,3,3]{2,1,0:T(4,128)}, u32[]{:S(2)}) copy-start(f32[3,3,3]{2,1,0:T(4,128)} %param.8) | copy-start | bytes 328
  147.6 9.2 %collective-permute-start.7 = (bf16[1,16,4096]{2,1,0:T(8,128)(2,1)S(1)}, bf16[1,16,4096]{2,1,0:T(8,128)(2,1)S(1)}, u32[]{:S(2)}, u32[]{:S(2)}) collective-permute-start(bf16[1,16,4096]{2,1,0:T(8,128)(2,1)S(1)} %bitcast.199), channel_id=1, source_target_pairs={{0,384},{64,448},{128,256},{192,320},{256,128},{320,192},{384,0},{... | collective-permute-start | bytes 393224 | tf_op jit(solution)/shard_map/ppermute | solution.py:25
  152.1 8.5 %collective-permute-start.8 = (bf16[1,16,4096]{2,1,0:T(8,128)(2,1)S(1)}, bf16[1,16,4096]{2,1,0:T(8,128)(2,1)S(1)}, u32[]{:S(2)}, u32[]{:S(2)}) collective-permute-start(bf16[1,16,4096]{2,1,0:T(8,128)(2,1)S(1)} %bitcast.198), channel_id=1, source_target_pairs={{0,448},{64,384},{128,320},{192,256},{256,192},{320,128},{384,64},... | collective-permute-start | bytes 393224 | tf_op jit(solution)/shard_map/ppermute | solution.py:25
  161.3 6.3 %collective-permute-start.10 = (bf16[8,16,1]{2,1,0:T(8,128)(2,1)S(1)}, bf16[8,16,1]{2,1,0:T(8,128)(2,1)S(1)}, u32[]{:S(2)}, u32[]{:S(2)}) collective-permute-start(bf16[8,16,1]{2,1,0:T(8,128)(2,1)S(1)} %get-tuple-element.11), channel_id=1, source_target_pairs={{64,0},{128,64},{192,128},{256,192},{320,256},{384,320},{448,384},... | collective-permute-start | bytes 776 | tf_op jit(solution)/shard_map/ppermute | solution.py:44
  163.6 4.3 %collective-permute-start.9 = (bf16[8,16,1]{2,1,0:T(8,128)(2,1)S(1)}, bf16[8,16,1]{2,1,0:T(8,128)(2,1)S(1)}, u32[]{:S(2)}, u32[]{:S(2)}) collective-permute-start(bf16[8,16,1]{2,1,0:T(8,128)(2,1)S(1)} %get-tuple-element.12), channel_id=1, source_target_pairs={{0,64},{64,128},{128,192},{192,256},{256,320},{320,384},{384,448},... | collective-permute-start | bytes 776 | tf_op jit(solution)/shard_map/ppermute | solution.py:43
  169.7 8.8 %collective-permute-start.11 = (bf16[8,1,4098]{2,1,0:T(2,128)(2,1)S(1)}, bf16[8,1,4098]{2,1,0:T(2,128)(2,1)S(1)}, u32[]{:S(2)}, u32[]{:S(2)}) collective-permute-start(bf16[8,1,4098]{2,1,0:T(2,128)(2,1)S(1)} %get-tuple-element.7), channel_id=1, source_target_pairs={{0,1},{1,2},{2,3},{3,4},{4,5},{5,6},{6,7},{7,8},{8,9},{9,10},{10,1... | collective-permute-start | bytes 196712 | tf_op jit(solution)/shard_map/ppermute | solution.py:43
  172.7 7.4 %collective-permute-start.12 = (bf16[8,1,4098]{2,1,0:T(2,128)(2,1)S(1)}, bf16[8,1,4098]{2,1,0:T(2,128)(2,1)S(1)}, u32[]{:S(2)}, u32[]{:S(2)}) collective-permute-start(bf16[8,1,4098]{2,1,0:T(2,128)(2,1)S(1)} %get-tuple-element.8), channel_id=1, source_target_pairs={{1,0},{2,1},{3,2},{4,3},{5,4},{6,5},{7,6},{8,7},{9,8},{10,9},{11,1... | collective-permute-start | bytes 196712 | tf_op jit(solution)/shard_map/ppermute | solution.py:44
  180.8 33.2 %copy-start.2 = (f32[3,3,3]{2,1,0:T(4,128)S(1)}, f32[3,3,3]{2,1,0:T(4,128)}, u32[]{:S(2)}) copy-start(f32[3,3,3]{2,1,0:T(4,128)} %param.9) | copy-start | bytes 328
  207.7 6.9 %collective-permute-start.13 = (bf16[8,16,1]{2,1,0:T(8,128)(2,1)S(1)}, bf16[8,16,1]{2,1,0:T(8,128)(2,1)S(1)}, u32[]{:S(2)}, u32[]{:S(2)}) collective-permute-start(bf16[8,16,1]{2,1,0:T(8,128)(2,1)S(1)} %get-tuple-element.10), channel_id=1, source_target_pairs={{0,64},{64,128},{128,192},{192,256},{256,320},{320,384},{384,448},... | collective-permute-start | bytes 776 | tf_op jit(solution)/shard_map/ppermute | solution.py:43
  212.0 5.2 %collective-permute-start.14 = (bf16[8,16,1]{2,1,0:T(8,128)(2,1)S(1)}, bf16[8,16,1]{2,1,0:T(8,128)(2,1)S(1)}, u32[]{:S(2)}, u32[]{:S(2)}) collective-permute-start(bf16[8,16,1]{2,1,0:T(8,128)(2,1)S(1)} %get-tuple-element.9), channel_id=1, source_target_pairs={{64,0},{128,64},{192,128},{256,192},{320,256},{384,320},{448,384},... | collective-permute-start | bytes 776 | tf_op jit(solution)/shard_map/ppermute | solution.py:44
  219.0 9.1 %collective-permute-start.15 = (bf16[8,1,4098]{2,1,0:T(2,128)(2,1)S(1)}, bf16[8,1,4098]{2,1,0:T(2,128)(2,1)S(1)}, u32[]{:S(2)}, u32[]{:S(2)}) collective-permute-start(bf16[8,1,4098]{2,1,0:T(2,128)(2,1)S(1)} %get-tuple-element.5), channel_id=1, source_target_pairs={{0,1},{1,2},{2,3},{3,4},{4,5},{5,6},{6,7},{7,8},{8,9},{9,10},{10,1... | collective-permute-start | bytes 196712 | tf_op jit(solution)/shard_map/ppermute | solution.py:43
  221.4 7.7 %collective-permute-start.16 = (bf16[8,1,4098]{2,1,0:T(2,128)(2,1)S(1)}, bf16[8,1,4098]{2,1,0:T(2,128)(2,1)S(1)}, u32[]{:S(2)}, u32[]{:S(2)}) collective-permute-start(bf16[8,1,4098]{2,1,0:T(2,128)(2,1)S(1)} %get-tuple-element.6), channel_id=1, source_target_pairs={{1,0},{2,1},{3,2},{4,3},{5,4},{6,5},{7,6},{8,7},{9,8},{10,9},{11,1... | collective-permute-start | bytes 196712 | tf_op jit(solution)/shard_map/ppermute | solution.py:44
